TPU v7x, 32 devices: a whole 2x2x4 slice. The times are simulated.
32 devices in a mesh: expert: 16 (over z, y, core), tensor: 2 (over x).
Axes of the slice: x: 2, y: 2, z: 4, core: 2. Of those that a mesh axis runs over, the one named last changes fastest.
Arguments:
- tokens: bfloat16 [18912, 768], P('expert'), may hold values from -6 to 6
- teacher: bfloat16 [18912, 768], P('expert'), may hold values from -12 to 12
- valid_flags: int32 [96], P('expert'), may hold values from 0 to 1, as said below
- routes: int32 [18912, 2], P('expert'), may hold values from 0 to 7, all different within a row; in each aligned block of 1182 rows (0 to 1181, 1182 to 2363, ...) at most 440 rows name the same one
- capacity: int32 [8], replicated, may hold values from 220 to 440, as said below
- norm_gains: bfloat16 [4, 768], replicated, may hold values from 0.5 to 1.5
- norm_biases: bfloat16 [4, 768], replicated, may hold values from -0.59765625 to 0.59765625
- attn_qkv: bfloat16 [2, 3, 768, 768], P(None, None, None, 'tensor'), may hold values from -0.21875 to 0.21875
- attn_out: bfloat16 [2, 768, 768], P(None, 'tensor'), may hold values from -1.75 to 1.75
- mlp_in: bfloat16 [768, 3072], P(None, 'tensor'), may hold values from -0.21875 to 0.21875
- mlp_out: bfloat16 [3072, 768], P('tensor'), may hold values from -0.109375 to 0.109375
- router: bfloat16 [768, 8], replicated, may hold values from -0.15625 to 0.15625
- expert_in: bfloat16 [16, 768, 1536], P('expert', None, 'tensor'), may hold values from -0.21875 to 0.21875
- expert_out: bfloat16 [16, 1536, 768], P('expert', 'tensor'), may hold values from -0.109375 to 0.109375
Outputs:
- activations: bfloat16 [18912, 768], P('expert')
- input_grad: bfloat16 [18912, 768], P('expert')
- gain_grad: float32 [4, 768], P(None, 'expert')
- bias_grad: float32 [3, 768], P(None, 'expert')
- expert_norm_bias_grad: float32 [768], P('expert')
- qkv_grad: float32 [2, 3, 768, 768], P(None, None, 'expert', 'tensor')
- out_proj_grad: float32 [2, 768, 768], P(None, 'tensor', 'expert')
- mlp_in_grad: float32 [768, 3072], P('expert', 'tensor')
- mlp_out_grad: float32 [3072, 768], P('tensor', 'expert')
- router_grad: float32 [768, 8], P('expert')
- expert_in_grad: float32 [16, 768, 1536], P('expert', None, 'tensor')
- expert_out_grad: float32 [16, 1536, 768], P('expert', 'tensor')
Inputs may be any that keep to these rules, and one draw needn't show every extreme that they name: `valid_flags`: 1 marks an image whose tokens count in the loss; image 0 is always valid. `routes`: the two experts of a token differ; among the rows of one index of expert no expert is named by more than 440 rows, and exactly 440 in some. `capacity`: exactly 440 for at least one expert.
All inputs are finite; a program needn't handle non-finite values.
Results may differ from a plain program's by a relative error of at most 0.035.
Values may be sent and summed in bfloat16 or wider, within the bound.
No kernel may reach another device: no remote copies, remote signals or barrier semaphores. Data moves between devices by JAX's collectives and lax.ppermute only.
A program may use at most 256 MiB of HBM per device.

v0:
```python
import jax
import jax.numpy as jnp
from jax import lax
from jax.sharding import PartitionSpec as P

HD = 64
SEQ = 197
IMG_DEV = 6
epsilon = 1e-06


def normalize(values, gain_row, bias_row):
    center = values - jnp.mean(values, axis=-1, keepdims=True)
    scaled = center * lax.rsqrt(jnp.mean(center * center, axis=-1, keepdims=True) + epsilon)
    return scaled * gain_row + bias_row


def norm_backward(values, gain_row, bias_row, grad_normed):
    pull_back = jax.vjp(normalize, values, gain_row, bias_row)[1]
    return pull_back(grad_normed)


def gelu_tanh(values):
    return jax.nn.gelu(values, approximate=True)


def tensor_total(partial_value):
    return lax.psum(partial_value.astype(jnp.bfloat16), "tensor").astype(jnp.float32)


def to_experts(buffer):
    doubled = jnp.repeat(buffer, 2, axis=0)
    arrived = lax.all_to_all(doubled, "expert", split_axis=0, concat_axis=0, tiled=True)
    return arrived


def from_experts(partial_value, experts):
    share_rows = lax.psum_scatter(
        partial_value.astype(jnp.bfloat16), "tensor", scatter_dimension=1, tiled=True
    )
    full_rows = lax.all_gather(share_rows, "tensor", axis=1, tiled=True)
    back_rows = lax.all_to_all(full_rows, "expert", split_axis=0, concat_axis=0, tiled=True)
    slots_each = back_rows.shape[1]
    halves = back_rows.reshape(experts, 2, slots_each, -1).astype(jnp.float32)
    return jnp.sum(halves, axis=1).reshape(experts * slots_each, -1)


def attend_forward(normed_low, qkv_weight, out_weight):
    packed = jnp.einsum(
        "td,sdc->stc", normed_low, qkv_weight, preferred_element_type=jnp.float32
    ).astype(jnp.bfloat16)
    heads_qkv = packed.reshape(3, IMG_DEV, SEQ, -1, HD)
    scores = jnp.einsum(
        "bqhe,bkhe->bhqk", heads_qkv[0], heads_qkv[1], preferred_element_type=jnp.float32
    ) * HD ** (-0.5)
    log_total = jax.nn.logsumexp(scores, axis=-1, keepdims=True)
    attn_probs = jnp.exp(scores - log_total).astype(jnp.bfloat16)
    mixed_rows = jnp.einsum(
        "bhqk,bkhe->bqhe", attn_probs, heads_qkv[2], preferred_element_type=jnp.float32
    )
    mixed_rows = mixed_rows.reshape(normed_low.shape[0], -1).astype(jnp.bfloat16)
    branch = jnp.dot(mixed_rows, out_weight, preferred_element_type=jnp.float32)
    return (branch, (packed, log_total, mixed_rows))


def attend_backward(grad_residual, normed_low, qkv_weight, out_weight, kept_state):
    packed, log_total, mixed_rows = kept_state
    grad_low = grad_residual.astype(jnp.bfloat16)
    grad_out = jnp.einsum("tc,td->cd", mixed_rows, grad_low, preferred_element_type=jnp.float32)
    heads_qkv = packed.reshape(3, IMG_DEV, SEQ, -1, HD)
    grad_mixed = jnp.einsum("td,cd->tc", grad_low, out_weight, preferred_element_type=jnp.float32)
    grad_mixed = grad_mixed.astype(jnp.bfloat16).reshape(heads_qkv.shape[1:])
    scores = jnp.einsum(
        "bqhe,bkhe->bhqk", heads_qkv[0], heads_qkv[1], preferred_element_type=jnp.float32
    ) * HD ** (-0.5)
    attn_probs = jnp.exp(scores - log_total)
    grad_probs = jnp.einsum(
        "bqhe,bkhe->bhqk", grad_mixed, heads_qkv[2], preferred_element_type=jnp.float32
    )
    grad_scores = attn_probs * (
        grad_probs - jnp.sum(grad_probs * attn_probs, axis=-1, keepdims=True)
    )
    grad_scores = grad_scores.astype(jnp.bfloat16)
    grad_query = jnp.einsum(
        "bhqk,bkhe->bqhe", grad_scores, heads_qkv[1], preferred_element_type=jnp.float32
    ) * HD ** (-0.5)
    grad_key = jnp.einsum(
        "bhqk,bqhe->bkhe", grad_scores, heads_qkv[0], preferred_element_type=jnp.float32
    ) * HD ** (-0.5)
    grad_value = jnp.einsum(
        "bhqk,bqhe->bkhe",
        attn_probs.astype(jnp.bfloat16),
        grad_mixed,
        preferred_element_type=jnp.float32,
    )
    grad_packed = (
        jnp.stack([grad_query, grad_key, grad_value]).reshape(packed.shape).astype(jnp.bfloat16)
    )
    grad_weight = jnp.einsum(
        "td,stc->sdc", normed_low, grad_packed, preferred_element_type=jnp.float32
    )
    grad_normed = jnp.einsum(
        "stc,sdc->td", grad_packed, qkv_weight, preferred_element_type=jnp.float32
    )
    return (grad_normed, grad_weight, grad_out)


def ffn_forward(rows_in, weight_in, weight_out):
    hidden = jnp.dot(rows_in, weight_in, preferred_element_type=jnp.float32)
    active = gelu_tanh(hidden).astype(jnp.bfloat16)
    return (jnp.dot(active, weight_out, preferred_element_type=jnp.float32), hidden, active)


def ffn_backward(grad_low, rows_in, weight_in, weight_out, hidden, active):
    grad_out = jnp.einsum("tf,td->fd", active, grad_low, preferred_element_type=jnp.float32)
    grad_active = jnp.einsum("td,fd->tf", grad_low, weight_out, preferred_element_type=jnp.float32)
    grad_hidden = jax.vjp(gelu_tanh, hidden)[1](grad_active)[0].astype(jnp.bfloat16)
    grad_in = jnp.einsum("td,tf->df", rows_in, grad_hidden, preferred_element_type=jnp.float32)
    grad_rows = jnp.einsum("tf,df->td", grad_hidden, weight_in, preferred_element_type=jnp.float32)
    return (grad_rows, grad_in, grad_out)


def body(
    tokens,
    teacher,
    valid_flags,
    routes,
    capacity,
    norm_gains,
    norm_biases,
    attn_qkv,
    attn_out,
    mlp_in,
    mlp_out,
    router,
    expert_in,
    expert_out,
):
    local_rows = tokens.shape[0]
    experts = router.shape[1]
    slots_each = 4 * (3 * local_rows // (4 * experts))
    all_slots = experts * slots_each
    owners = lax.axis_size("expert")
    gain_rows = norm_gains.astype(jnp.float32)
    bias_rows = norm_biases.astype(jnp.float32)
    local_count = SEQ * jnp.sum(valid_flags.astype(jnp.float32))
    valid_count = lax.psum(local_count, "expert")
    valid_rows = jnp.repeat(valid_flags.astype(jnp.float32), SEQ)[:, None]
    start_rows = tokens.astype(jnp.float32)
    normed_first = normalize(start_rows, gain_rows[0], bias_rows[0]).astype(jnp.bfloat16)
    branch, saved_first = attend_forward(normed_first, attn_qkv[0], attn_out[0])
    after_attn = start_rows + tensor_total(branch)
    normed_dense = normalize(after_attn, gain_rows[1], bias_rows[1]).astype(jnp.bfloat16)
    branch, dense_hidden, dense_active = ffn_forward(normed_dense, mlp_in, mlp_out)
    after_dense = after_attn + tensor_total(branch)
    normed_second = normalize(after_dense, gain_rows[2], bias_rows[2]).astype(jnp.bfloat16)
    branch, saved_second = attend_forward(normed_second, attn_qkv[1], attn_out[1])
    after_second = after_dense + tensor_total(branch)
    normed_expert = normalize(after_second, gain_rows[3], bias_rows[3]).astype(jnp.bfloat16)
    logits = jnp.dot(normed_expert, router, preferred_element_type=jnp.float32)
    picker = routes[:, :, None] == jnp.arange(experts, dtype=jnp.int32)[None, None, :]
    chosen = jnp.sum(jnp.where(picker, logits[:, None, :], 0.0), axis=2)
    gate_vals = jax.nn.softmax(chosen, axis=1)
    expert_of = jnp.concatenate([routes[:, 0], routes[:, 1]])
    onehot = (expert_of[:, None] == jnp.arange(experts, dtype=jnp.int32)[None, :]).astype(jnp.int32)
    earlier = jnp.cumsum(onehot, axis=0) - onehot
    position = jnp.sum(earlier * onehot, axis=1)
    kept_mask = position < jnp.sum(onehot * capacity[None, :], axis=1)
    slot_of = expert_of * slots_each + position
    pair_of = (
        jnp.full((all_slots,), -1, jnp.int32)
        .at[jnp.where(kept_mask, slot_of, all_slots)]
        .set(jnp.arange(2 * local_rows, dtype=jnp.int32), mode="drop")
    )
    slot_used = (pair_of >= 0)[:, None]
    pair_index = jnp.maximum(pair_of, 0)
    fetch_at = jnp.where(kept_mask, slot_of, 0)
    sent_rows = jnp.where(
        slot_used, normed_expert[pair_index % local_rows], jnp.zeros((), jnp.bfloat16)
    )
    rows_in = to_experts(sent_rows.reshape(experts, slots_each, -1)).reshape(
        owners * slots_each, -1
    )
    branch, expert_hidden, expert_active = ffn_forward(rows_in, expert_in[0], expert_out[0])
    merged = from_experts(branch.reshape(owners, slots_each, -1), experts)
    picked = jnp.where(kept_mask[:, None], merged[fetch_at], 0.0).reshape(2, local_rows, -1)
    gate_pairs = gate_vals.T[:, :, None]
    final_rows = after_second + jnp.sum(gate_pairs * picked, axis=0)
    grad_final = (
        local_rows * owners / valid_count * valid_rows * (final_rows - teacher.astype(jnp.float32))
    )
    grad_gates = jnp.sum(picked * grad_final[None], axis=2).T
    grad_pairs = (gate_pairs * grad_final[None]).astype(jnp.bfloat16).reshape(2 * local_rows, -1)
    grad_sent = jnp.where(slot_used, grad_pairs[pair_index], jnp.zeros((), jnp.bfloat16))
    grad_arrived = to_experts(grad_sent.reshape(experts, slots_each, -1)).reshape(
        owners * slots_each, -1
    )
    grad_rows, grad_expert_in, grad_expert_out = ffn_backward(
        grad_arrived, rows_in, expert_in[0], expert_out[0], expert_hidden, expert_active
    )
    grad_merged = from_experts(grad_rows.reshape(owners, slots_each, -1), experts)
    grad_taken = jnp.where(kept_mask[:, None], grad_merged[fetch_at], 0.0).reshape(
        2, local_rows, -1
    )
    grad_chosen = gate_vals * (grad_gates - jnp.sum(gate_vals * grad_gates, axis=1, keepdims=True))
    grad_logits = jnp.sum(jnp.where(picker, grad_chosen[:, :, None], 0.0), axis=1).astype(
        jnp.bfloat16
    )
    grad_router = jnp.einsum(
        "td,te->de", normed_expert, grad_logits, preferred_element_type=jnp.float32
    )
    grad_normed = jnp.sum(grad_taken, axis=0)
    grad_normed = grad_normed + jnp.einsum(
        "te,de->td", grad_logits, router, preferred_element_type=jnp.float32
    )
    grad_back, gain_four, bias_four = norm_backward(
        after_second, gain_rows[3], bias_rows[3], grad_normed
    )
    grad_second = grad_final + grad_back
    grad_part, qkv_two, out_two = attend_backward(
        grad_second, normed_second, attn_qkv[1], attn_out[1], saved_second
    )
    grad_back, gain_three, bias_three = norm_backward(
        after_dense, gain_rows[2], bias_rows[2], tensor_total(grad_part)
    )
    grad_dense = grad_second + grad_back
    grad_part, grad_mlp_in, grad_mlp_out = ffn_backward(
        grad_dense.astype(jnp.bfloat16), normed_dense, mlp_in, mlp_out, dense_hidden, dense_active
    )
    grad_back, gain_two, bias_two = norm_backward(
        after_attn, gain_rows[1], bias_rows[1], tensor_total(grad_part)
    )
    grad_attn = grad_dense + grad_back
    grad_part, qkv_one, out_one = attend_backward(
        grad_attn, normed_first, attn_qkv[0], attn_out[0], saved_first
    )
    grad_back, gain_one, bias_one = norm_backward(
        start_rows, gain_rows[0], bias_rows[0], tensor_total(grad_part)
    )
    grad_start = grad_attn + grad_back
    summed = (
        lax.psum_scatter(
            jnp.stack([gain_one, gain_two, gain_three, gain_four]),
            "expert",
            scatter_dimension=1,
            tiled=True,
        ),
        lax.psum_scatter(
            jnp.stack([bias_one, bias_two, bias_three]), "expert", scatter_dimension=1, tiled=True
        ),
        lax.psum_scatter(bias_four, "expert", scatter_dimension=0, tiled=True),
        lax.psum_scatter(jnp.stack([qkv_one, qkv_two]), "expert", scatter_dimension=2, tiled=True),
        lax.psum_scatter(jnp.stack([out_one, out_two]), "expert", scatter_dimension=2, tiled=True),
        lax.psum_scatter(grad_mlp_in, "expert", scatter_dimension=0, tiled=True),
        lax.psum_scatter(grad_mlp_out, "expert", scatter_dimension=1, tiled=True),
        lax.psum_scatter(grad_router, "expert", scatter_dimension=0, tiled=True),
    )
    return (
        final_rows.astype(jnp.bfloat16),
        grad_start.astype(jnp.bfloat16),
        summed[0],
        summed[1],
        summed[2],
        summed[3],
        summed[4],
        summed[5],
        summed[6],
        summed[7],
        grad_expert_in[None],
        grad_expert_out[None],
    )


def solution(mesh):
    in_specs = (
        P("expert", None),
        P("expert", None),
        P("expert"),
        P("expert", None),
        P(),
        P(),
        P(),
        P(None, None, None, "tensor"),
        P(None, "tensor", None),
        P(None, "tensor"),
        P("tensor", None),
        P(),
        P("expert", None, "tensor"),
        P("expert", "tensor", None),
    )
    out_specs = (
        P("expert", None),
        P("expert", None),
        P(None, "expert"),
        P(None, "expert"),
        P("expert"),
        P(None, None, "expert", "tensor"),
        P(None, "tensor", "expert"),
        P("expert", "tensor"),
        P("tensor", "expert"),
        P("expert", None),
        P("expert", None, "tensor"),
        P("expert", "tensor", None),
    )
    return jax.shard_map(body, mesh=mesh, in_specs=in_specs, out_specs=out_specs, check_vma=False)
```

profile of v0, /device:TPU:0, one launch (start us, length us, event | category | flops | bytes accessed | tf_op | source)
XLA Modules:
  0.0 2914.6 jit_solution(6737565340386454107)
XLA Ops:
  57.4 59.4 %all-reduce.13.cloned.1.call-done = bf16[1182,768]{1,0:T(8,128)(2,1)} async-done(((bf16[1182,768]{1,0:T(8,128)(2,1)}), bf16[1182,768]{1,0:T(8,128)(2,1)}) %all-reduce.13.cloned.1.call-update) | async-done | bytes 1815568 | tf_op jit(solution)/shard_map/psum | solution.py:28
  133.9 56.3 %all-reduce.15.cloned.1.call-done = bf16[1182,768]{1,0:T(8,128)(2,1)} async-done(((bf16[1182,768]{1,0:T(8,128)(2,1)}), bf16[1182,768]{1,0:T(8,128)(2,1)}) %all-reduce.15.cloned.1.call-update) | async-done | bytes 1815568 | tf_op jit(solution)/shard_map/psum | solution.py:28
  242.7 12.3 scatter_custom_fusion
  255.7 40.5 %all-reduce.17.cloned.1.call-done = bf16[1182,768]{1,0:T(8,128)(2,1)} async-done(((bf16[1182,768]{1,0:T(8,128)(2,1)}), bf16[1182,768]{1,0:T(8,128)(2,1)}) %all-reduce.17.cloned.1.call-update) | async-done | bytes 1815568 | tf_op jit(solution)/shard_map/psum | solution.py:28
  302.3 15.6 gather_fusion
  322.4 240.6 %all_to_all.20 = bf16[16,440,768]{2,1,0:T(8,128)(2,1)} all-to-all(bf16[16,440,768]{2,1,0:T(8,128)(2,1)S(1)} %bitcast.188), channel_id=1, replica_groups=mesh['expert'=16,'tensor'=2] {'expert'}, dimensions={0} | all-to-all | bytes 21626880 | tf_op jit(solution)/shard_map/all_to_all | solution.py:33
  562.9 20.0 multiply_convert_fusion
  582.9 13.2 convolution_convert_fusion.1
  605.2 125.0 %reduce-scatter.14.cloned.1.call-done = bf16[16,220,768]{2,0,1:T(8,128)(2,1)} async-done(((bf16[16,440,768]{2,0,1:T(8,128)(2,1)}), bf16[16,220,768]{2,0,1:T(8,128)(2,1)}) %reduce-scatter.14.cloned.1.call-update) | async-done | bytes 5406736 | tf_op jit(solution)/shard_map/reduce_scatter | solution.py:38
  730.3 134.6 %all-gather.3.cloned.1.call-done = bf16[16,440,768]{2,0,1:T(8,128)(2,1)} async-done(((bf16[16,220,768]{2,0,1:T(8,128)(2,1)}), bf16[16,440,768]{2,0,1:T(8,128)(2,1)}) %all-gather.3.cloned.1.call-update) | async-done | bytes 10813456 | tf_op jit(solution)/shard_map/all_gather | solution.py:41
  864.9 12.0 copy.243
  884.0 211.2 %psum.52 = f32[]{:T(128)} all-reduce(f32[]{:T(128)S(6)} %mul_shard_map.3), channel_id=1, replica_groups=mesh['expert'=16,'tensor'=2] {'expert'}, use_global_device_ids=true, to_apply=%region_27.28 | all-reduce | flops 1 | bytes 8 | tf_op jit(solution)/shard_map/psum | solution.py:147
  1110.1 14.3 gather_fusion.1
  1157.9 16.4 gather_fusion.2
  1178.7 279.8 %all_to_all.21 = bf16[16,440,768]{2,1,0:T(8,128)(2,1)S(1)} all-to-all(bf16[16,440,768]{2,1,0:T(8,128)(2,1)S(1)} %bitcast.189), channel_id=1, replica_groups=mesh['expert'=16,'tensor'=2] {'expert'}, dimensions={0} | all-to-all | bytes 21626880 | tf_op jit(solution)/shard_map/all_to_all | solution.py:33
  1458.5 28.1 fusion.6
  1507.7 125.0 %reduce-scatter.16.cloned.1.call-done = bf16[16,220,768]{2,0,1:T(8,128)(2,1)} async-done(((bf16[16,440,768]{2,0,1:T(8,128)(2,1)}), bf16[16,220,768]{2,0,1:T(8,128)(2,1)}) %reduce-scatter.16.cloned.1.call-update) | async-done | bytes 5406736 | tf_op jit(solution)/shard_map/reduce_scatter | solution.py:38
  1632.7 134.7 %all-gather.5.cloned.1.call-done = bf16[16,440,768]{2,0,1:T(8,128)(2,1)} async-done(((bf16[16,220,768]{2,0,1:T(8,128)(2,1)}), bf16[16,440,768]{2,0,1:T(8,128)(2,1)}) %all-gather.5.cloned.1.call-update) | async-done | bytes 10813456 | tf_op jit(solution)/shard_map/all_gather | solution.py:41
  1767.4 12.4 copy.247
  1785.9 192.7 %all-to-all-done.3 = bf16[16,440,768]{2,1,0:T(8,128)(2,1)} async-done(((bf16[16,440,768]{2,1,0:T(8,128)(2,1)}), bf16[16,440,768]{2,1,0:T(8,128)(2,1)}, u32[]{:S(2)}, u32[]{:S(2)}) %all-to-all-start.3) | async-done | bytes 10813472 | tf_op jit(solution)/shard_map/all_to_all | solution.py:42
  1989.5 14.2 gather_fusion.3
  2079.2 97.6 %all-reduce.19.cloned.1.call-done = bf16[1182,768]{1,0:T(8,128)(2,1)} async-done(((bf16[1182,768]{1,0:T(8,128)(2,1)}), bf16[1182,768]{1,0:T(8,128)(2,1)}) %all-reduce.19.cloned.1.call-update) | async-done | bytes 1815568 | tf_op jit(solution)/shard_map/psum | solution.py:28
  2199.3 57.0 %all-reduce.21.cloned.1.call-done = bf16[1182,768]{1,0:T(8,128)(2,1)} async-done(((bf16[1182,768]{1,0:T(8,128)(2,1)}), bf16[1182,768]{1,0:T(8,128)(2,1)}) %all-reduce.21.cloned.1.call-update) | async-done | bytes 1815568 | tf_op jit(solution)/shard_map/psum | solution.py:28
  2348.3 35.2 %all-reduce.23.cloned.1.call-done = bf16[1182,768]{1,0:T(8,128)(2,1)} async-done(((bf16[1182,768]{1,0:T(8,128)(2,1)}), bf16[1182,768]{1,0:T(8,128)(2,1)}) %all-reduce.23.cloned.1.call-update) | async-done | bytes 1815568 | tf_op jit(solution)/shard_map/psum | solution.py:28
  2399.0 13.6 copy.280
  2444.6 14.6 convolution_bitcast_fusion.5
  2459.2 14.7 convolution_bitcast_fusion.4
  2473.9 29.6 %all-reduce.1 = f32[768]{0:T(1024)S(1)} all-reduce(f32[768]{0:T(1024)S(1)} %copy-done.118), channel_id=6, replica_groups=mesh['expert'=16,'tensor'=2] {'expert'}, use_global_device_ids=true, to_apply=%region_57.58.clone | all-reduce | flops 768 | bytes 6144
  2510.2 50.1 %reduce-scatter.22.cloned.1.call-done = f32[48,4]{1,0:T(8,128)} async-done(((f32[768,4]{1,0:T(8,128)}), f32[48,4]{1,0:T(8,128)}) %reduce-scatter.22.cloned.1.call-update) | async-done | bytes 784
  2561.6 186.9 %all-reduce.25.cloned.1.call-done = (f32[2,3,768,384]{3,0,1,2:T(2,128)}, f32[2,384,768]{1,0,2:T(2,128)}) async-done(((f32[2,3,768,384]{3,0,1,2:T(2,128)}, f32[2,384,768]{1,0,2:T(2,128)}), (f32[2,3,768,384]{3,0,1,2:T(2,128)}, f32[2,384,768]{1,0,2:T(2,128)})) %all-reduce.25.cloned.1.call-update) | async-done | bytes 9437200
  2752.1 76.4 %reduce-scatter.18.cloned.1.call-done = f32[48,1536]{1,0:T(8,128)} async-done(((f32[768,1536]{1,0:T(8,128)}), f32[48,1536]{1,0:T(8,128)}) %reduce-scatter.18.cloned.1.call-update) | async-done | bytes 294928 | tf_op jit(solution)/shard_map/reduce_scatter | solution.py:254
  2828.4 79.4 %reduce-scatter.20.cloned.1.call-done = f32[1536,48]{0,1:T(8,128)} async-done(((f32[1536,768]{0,1:T(8,128)}), f32[1536,48]{0,1:T(8,128)}) %reduce-scatter.20.cloned.1.call-update) | async-done | bytes 294928 | tf_op jit(solution)/shard_map/reduce_scatter | solution.py:255
  (535 shorter events, 483.5 us)
Async XLA Ops:
  7.2 120.6 %copy-start = (bf16[1536,768]{1,0:T(8,128)(2,1)S(1)}, bf16[1536,768]{1,0:T(8,128)(2,1)}, u32[]{:S(2)}) copy-start(bf16[1536,768]{1,0:T(8,128)(2,1)} %param.24) | copy-start | bytes 7077892
  7.2 109.7 %all-reduce.13.cloned.1.call-start = ((), (), s32[]{:S(2)}) async-start(), calls=%async_computation.11 | async-start | bytes 3637248 | tf_op jit(solution)/shard_map/psum | solution.py:28
  13.6 107.9 %copy-start.104 = (f32[768]{0:T(1024)}, f32[768]{0:T(1024)S(1)}, u32[]{:S(2)}) copy-start(f32[768]{0:T(1024)S(1)} %get-tuple-element.135) | copy-start | bytes 9220
  13.6 286.2 %copy-start.98 = (f32[768]{0:T(1024)}, f32[768]{0:T(1024)S(1)}, u32[]{:S(2)}) copy-start(f32[768]{0:T(1024)S(1)} %get-tuple-element.137) | copy-start | bytes 9220
  57.2 64.3 %copy-start.126 = (f32[768]{0:T(1024)S(1)}, f32[768]{0:T(1024)}, u32[]{:S(2)}) copy-start(f32[768]{0:T(1024)} %get-tuple-element.97) | copy-start | bytes 9220
  57.2 133.0 %all-reduce.15.cloned.1.call-start = ((), (), s32[]{:S(2)}) async-start(), calls=%async_computation.12 | async-start | bytes 3637248 | tf_op jit(solution)/shard_map/psum | solution.py:28
  133.2 163.0 %all-reduce.17.cloned.1.call-start = ((), (), s32[]{:S(2)}) async-start(), calls=%async_computation.13 | async-start | bytes 3637248 | tf_op jit(solution)/shard_map/psum | solution.py:28
  239.2 491.1 %reduce-scatter.14.cloned.1.call-start = ((), (), s32[]{:S(2)}) async-start(), calls=%async_computation.14 | async-start | bytes 16220160 | tf_op jit(solution)/shard_map/reduce_scatter | solution.py:38
  322.3 240.6 %copy-start.140 = (bf16[1,768,768]{2,1,0:T(8,128)(2,1)S(1)}, bf16[1,768,768]{2,1,0:T(8,128)(2,1)}, u32[]{:S(2)}) copy-start(bf16[1,768,768]{2,1,0:T(8,128)(2,1)} %param.26) | copy-start | bytes 3538948
  605.2 259.7 %all-gather.3.cloned.1.call-start = ((), (), s32[]{:S(2)}) async-start(), calls=%async_computation.15 | async-start | bytes 16220160 | tf_op jit(solution)/shard_map/all_gather | solution.py:41
  876.9 219.3 %copy-start.110 = (bf16[768,8]{0,1:T(8,128)(2,1)S(1)}, bf16[768,8]{0,1:T(8,128)(2,1)}, u32[]{:S(2)}) copy-start(bf16[768,8]{0,1:T(8,128)(2,1)} %param.25) | copy-start | bytes 36868
  876.9 221.3 %copy-start.75 = (s32[1182,2]{0,1:T(2,128)S(1)}, s32[1182,2]{0,1:T(2,128)}, u32[]{:S(2)}) copy-start(s32[1182,2]{0,1:T(2,128)} %param.17) | copy-start | bytes 28372
  876.9 222.2 %all-to-all-start.1 = ((bf16[16,440,768]{2,1,0:T(8,128)(2,1)}), bf16[16,440,768]{2,1,0:T(8,128)(2,1)}, u32[]{:S(2)}, u32[]{:S(2)}) async-start(bf16[16,440,768]{2,1,0:T(8,128)(2,1)} %copy.243), calls=%async_computation.2 | async-start | bytes 21626880 | tf_op jit(solution)/shard_map/all_to_all | solution.py:42
  882.7 750.0 %reduce-scatter.16.cloned.1.call-start = ((), (), s32[]{:S(2)}) async-start(), calls=%async_computation.16 | async-start | bytes 16220160 | tf_op jit(solution)/shard_map/reduce_scatter | solution.py:38
  1178.7 279.8 %copy-start.139 = (bf16[1,768,768]{2,1,0:T(8,128)(2,1)S(1)}, bf16[1,768,768]{2,1,0:T(8,128)(2,1)}, u32[]{:S(2)}) copy-start(bf16[1,768,768]{2,1,0:T(8,128)(2,1)} %param.27) | copy-start | bytes 3538948
  1507.7 259.8 %all-gather.5.cloned.1.call-start = ((), (), s32[]{:S(2)}) async-start(), calls=%async_computation.17 | async-start | bytes 16220160 | tf_op jit(solution)/shard_map/all_gather | solution.py:41
  1779.9 198.7 %all-to-all-start.3 = ((bf16[16,440,768]{2,1,0:T(8,128)(2,1)}), bf16[16,440,768]{2,1,0:T(8,128)(2,1)}, u32[]{:S(2)}, u32[]{:S(2)}) async-start(bf16[16,440,768]{2,1,0:T(8,128)(2,1)} %copy.247), calls=%async_computation.5 | async-start | bytes 21626880 | tf_op jit(solution)/shard_map/all_to_all | solution.py:42
  1785.7 391.1 %all-reduce.19.cloned.1.call-start = ((), (), s32[]{:S(2)}) async-start(), calls=%async_computation.18 | async-start | bytes 3637248 | tf_op jit(solution)/shard_map/psum | solution.py:28
  1785.9 228.6 %copy-start.68 = (bf16[1182,8]{0,1:T(8,128)(2,1)}, bf16[1182,8]{0,1:T(8,128)(2,1)S(1)}, u32[]{:S(2)}) copy-start(bf16[1182,8]{0,1:T(8,128)(2,1)S(1)} %select_reduce_fusion.1) | copy-start | bytes 56740
  2073.6 103.2 %copy-start.67 = (f32[1182]{0:T(1024)S(1)}, f32[1182]{0:T(1024)}, u32[]{:S(2)}) copy-start(f32[1182]{0:T(1024)} %copy-done.66) | copy-start | bytes 14188
  2073.6 103.2 %copy-start.108 = (f32[768]{0:T(1024)S(1)}, f32[768]{0:T(1024)}, u32[]{:S(2)}) copy-start(f32[768]{0:T(1024)} %get-tuple-element.136) | copy-start | bytes 9220
  2079.2 102.2 %copy-start.82 = (f32[1182]{0:T(1024)S(1)}, f32[1182]{0:T(1024)}, u32[]{:S(2)}) copy-start(f32[1182]{0:T(1024)} %copy-done.81) | copy-start | bytes 14188
  2079.2 102.2 %copy-start.95 = (f32[1182]{0:T(1024)S(1)}, f32[1182]{0:T(1024)}, u32[]{:S(2)}) copy-start(f32[1182]{0:T(1024)} %copy-done.94) | copy-start | bytes 14188
  2079.2 177.0 %all-reduce.21.cloned.1.call-start = ((), (), s32[]{:S(2)}) async-start(), calls=%async_computation.19 | async-start | bytes 3637248 | tf_op jit(solution)/shard_map/psum | solution.py:28
  2199.2 61.8 %copy-start.92 = (f32[1182]{0:T(1024)S(1)}, f32[1182]{0:T(1024)}, u32[]{:S(2)}) copy-start(f32[1182]{0:T(1024)} %copy-done.91) | copy-start | bytes 14188
  2199.2 184.3 %all-reduce.23.cloned.1.call-start = ((), (), s32[]{:S(2)}) async-start(), calls=%async_computation.20 | async-start | bytes 3637248 | tf_op jit(solution)/shard_map/psum | solution.py:28
  2326.5 116.7 %reduce-scatter.26.cloned.1.call-start = ((), (), s32[]{:S(2)}) async-start(), calls=%async_computation.25 | async-start | bytes 417792
  2329.5 179.3 %reduce-scatter.24.cloned.1.call-start = ((), (), s32[]{:S(2)}) async-start(), calls=%async_computation.24 | async-start | bytes 417792
  2393.0 167.2 %reduce-scatter.22.cloned.1.call-start = ((), (), s32[]{:S(2)}) async-start(), calls=%async_computation.23 | async-start | bytes 417792
  2396.1 352.4 %all-reduce.25.cloned.1.call-start = ((), (), s32[]{:S(2)}) async-start(), calls=%async_computation.26 | async-start | bytes 18874368
  2418.0 410.5 %reduce-scatter.18.cloned.1.call-start = ((), (), s32[]{:S(2)}) async-start(), calls=%async_computation.21 | async-start | bytes 5013504 | tf_op jit(solution)/shard_map/reduce_scatter | solution.py:254
  2427.5 480.3 %reduce-scatter.20.cloned.1.call-start = ((), (), s32[]{:S(2)}) async-start(), calls=%async_computation.22 | async-start | bytes 5013504 | tf_op jit(solution)/shard_map/reduce_scatter | solution.py:255
  (137 other events, 986.0 us)
Sparse Core Ops, SparseCore 0:
  57.3 59.5 all-reduce.12
  133.3 56.8 all-reduce.14
  239.3 56.8 all-reduce.16
  605.3 124.8 reduce-scatter.13
  731.7 133.0 all-gather.2
  1507.8 124.8 reduce-scatter.15
  1634.2 133.1 all-gather.4
  2079.3 97.4 all-reduce.18
  2199.3 56.8 all-reduce.20
  2326.6 56.8 all-reduce.22
  2387.6 55.5 reduce-scatter.25
  2446.9 54.6 reduce-scatter.23
  2505.7 54.5 reduce-scatter.21
  2564.3 184.1 all-reduce.24
  2752.8 75.6 reduce-scatter.17
  2833.2 74.5 reduce-scatter.19
where the time goes:
time: 2920 us; the launch traced here: 2910 us
  waiting for transfers between devices  1450 us (50%)
  blocking collectives  761 us (26%)
  local copies, waits for them, and re-layouts  324 us (11%)
  matrix products  221 us (8%)
  other arithmetic  123 us (4%)
    all_to_all x2, blocking collectives, to_experts(): lax.all_to_all(doubled, 'expert', split_axis=0, concat_axis=0, tiled=True)  520 us
    psum x6, waiting for transfers between devices, tensor_total(): lax.psum(partial_value.astype(jnp.bfloat16), 'tensor').astype(jnp.float32)  346 us
    all_gather x2, waiting for transfers between devices, from_experts(): full_rows = lax.all_gather(share_rows, 'tensor', axis=1, tiled=True)  269 us
    reduce_scatter x2, waiting for transfers between devices, from_experts(): lax.psum_scatter(partial_value.astype(jnp.bfloat16), 'tensor', scatter_di...  250 us
    unnamed x20, waiting for transfers between devices  241 us
    psum x1, blocking collectives, body(): valid_count = lax.psum(local_count, 'expert')  211 us
    all_to_all x2, waiting for transfers between devices, from_experts(): lax.all_to_all(full_rows, 'expert', split_axis=0, concat_axis=0, tiled=True)  193 us
    reduce_scatter x1, waiting for transfers between devices, body(): lax.psum_scatter(grad_mlp_out, 'expert', scatter_dimension=1, tiled=True)  79.4 us
  transfers between devices with their start and end apart: 18, of which 16 were waited for; matrix products, arithmetic and copies ran while one was open for 5% of the time, Pallas kernels for 0%

commit v1 on v0

--- a/solution.py
+++ b/solution.py
@@ -9,6 +9,18 @@
 epsilon = 1e-06
 
 
+def exchange_directly(x, axis, split, join):
+    ways, here = (lax.axis_size(axis), lax.axis_index(axis))
+    width = x.shape[split] // ways
+    turned = jnp.roll(x, -here * width, axis=split)
+    got = [lax.slice_in_dim(turned, 0, width, axis=split)]
+    for far in range(1, ways):
+        sent = lax.slice_in_dim(turned, far * width, (far + 1) * width, axis=split)
+        got.append(lax.ppermute(sent, axis, [(d, (d + far) % ways) for d in range(ways)]))
+    line = jnp.concatenate(got[::-1], axis=join)
+    return jnp.roll(line, (here + 1) * got[0].shape[join], axis=join)
+
+
 def normalize(values, gain_row, bias_row):
     center = values - jnp.mean(values, axis=-1, keepdims=True)
     scaled = center * lax.rsqrt(jnp.mean(center * center, axis=-1, keepdims=True) + epsilon)
@@ -39,7 +51,7 @@
         partial_value.astype(jnp.bfloat16), "tensor", scatter_dimension=1, tiled=True
     )
     full_rows = lax.all_gather(share_rows, "tensor", axis=1, tiled=True)
-    back_rows = lax.all_to_all(full_rows, "expert", split_axis=0, concat_axis=0, tiled=True)
+    back_rows = exchange_directly(full_rows, "expert", 0, 0)
     slots_each = back_rows.shape[1]
     halves = back_rows.reshape(experts, 2, slots_each, -1).astype(jnp.float32)
     return jnp.sum(halves, axis=1).reshape(experts * slots_each, -1)

time: 2920 us -> 3470 us (1.19)
  local copies, waits for them, and re-layouts: 324 us -> 674 us
  other arithmetic: 123 us -> 327 us
  blocking collectives: 761 us -> 642 us
  starting transfers between devices: 12.7 us -> 99.5 us
    ppermute x0 -> x30, waiting for transfers between devices: none -> 245 us  [exchange_directly(): lax.ppermute(sent, axis, [(d, (d + far) % ways) for d in range(ways)])]
    all_to_all x2 -> x0, waiting for transfers between devices: 193 us -> none  [from_experts(): lax.all_to_all(full_rows, 'expert', split_axis=0, concat_axis=0, tiled=True)]
    reduce_sum x2, other arithmetic: 21.9 us -> 173 us  [from_experts(): return jnp.sum(halves, axis=1).reshape(experts * slots_each, -1)]
    concatenate x0 -> x2, local copies, waits for them, and re-layouts: none -> 116 us  [exchange_directly(): line = jnp.concatenate(got[::-1], axis=join)]
    ppermute x0 -> x30, starting transfers between devices: none -> 98.3 us  [exchange_directly(): lax.ppermute(sent, axis, [(d, (d + far) % ways) for d in range(ways)])]
    slice x1 -> x33, local copies, waits for them, and re-layouts: 0.3 us -> 98.5 us  [the longest x2 73 us: exchange_directly(): got = [lax.slice_in_dim(turned, 0, width, axis=split)]]
    ppermute x0 -> x30, local copies, waits for them, and re-layouts: none -> 89.5 us  [exchange_directly(): lax.ppermute(sent, axis, [(d, (d + far) % ways) for d in range(ways)])]
    psum x1, blocking collectives: 211 us -> 134 us  [body(): valid_count = lax.psum(local_count, 'expert')]
  transfers between devices with their start and end apart: 18 -> 46, of which waited for: 16 -> 29; matrix products, arithmetic and copies ran while one was open for 5% -> 7% of each run, Pallas kernels for 0% -> 0%
where the time goes in v1:
time: 3470 us; the launch traced here: 3450 us
  waiting for transfers between devices  1460 us (42%)
  local copies, waits for them, and re-layouts  674 us (19%)
  blocking collectives  642 us (19%)
  other arithmetic  327 us (9%)
  matrix products  224 us (6%)
  starting transfers between devices  99.5 us (3%)
    all_to_all x2, blocking collectives, to_experts(): lax.all_to_all(doubled, 'expert', split_axis=0, concat_axis=0, tiled=True)  479 us
    psum x6, waiting for transfers between devices, tensor_total(): lax.psum(partial_value.astype(jnp.bfloat16), 'tensor').astype(jnp.float32)  304 us
    all_gather x2, waiting for transfers between devices, from_experts(): full_rows = lax.all_gather(share_rows, 'tensor', axis=1, tiled=True)  269 us
    reduce_scatter x2, waiting for transfers between devices, from_experts(): lax.psum_scatter(partial_value.astype(jnp.bfloat16), 'tensor', scatter_di...  249 us
    ppermute x30, waiting for transfers between devices, exchange_directly(): lax.ppermute(sent, axis, [(d, (d + far) % ways) for d in range(ways)])  245 us
    unnamed x20, waiting for transfers between devices  241 us
    reduce_sum x2, other arithmetic, from_experts(): return jnp.sum(halves, axis=1).reshape(experts * slots_each, -1)  173 us
    psum x1, blocking collectives, body(): valid_count = lax.psum(local_count, 'expert')  134 us
  transfers between devices with their start and end apart: 46, of which 29 were waited for; matrix products, arithmetic and copies ran while one was open for 7% of the time, Pallas kernels for 0%

profile of v1, /device:TPU:0, one launch (start us, length us, event | category | flops | bytes accessed | tf_op | source)
XLA Modules:
  0.0 3448.8 jit_solution(12692426500911778415)
XLA Ops:
  56.1 59.5 %all-reduce.13.cloned.1.call-done = bf16[1182,768]{1,0:T(8,128)(2,1)} async-done(((bf16[1182,768]{1,0:T(8,128)(2,1)}), bf16[1182,768]{1,0:T(8,128)(2,1)}) %all-reduce.13.cloned.1.call-update) | async-done | bytes 1815568 | tf_op jit(solution)/shard_map/psum | solution.py:40
  132.6 56.3 %all-reduce.15.cloned.1.call-done = bf16[1182,768]{1,0:T(8,128)(2,1)} async-done(((bf16[1182,768]{1,0:T(8,128)(2,1)}), bf16[1182,768]{1,0:T(8,128)(2,1)}) %all-reduce.15.cloned.1.call-update) | async-done | bytes 1815568 | tf_op jit(solution)/shard_map/psum | solution.py:40
  254.6 40.2 %all-reduce.17.cloned.1.call-done = bf16[1182,768]{1,0:T(8,128)(2,1)} async-done(((bf16[1182,768]{1,0:T(8,128)(2,1)}), bf16[1182,768]{1,0:T(8,128)(2,1)}) %all-reduce.17.cloned.1.call-update) | async-done | bytes 1815568 | tf_op jit(solution)/shard_map/psum | solution.py:40
  321.0 240.6 %all_to_all.10 = bf16[16,440,768]{2,1,0:T(8,128)(2,1)} all-to-all(bf16[16,440,768]{2,1,0:T(8,128)(2,1)S(1)} %bitcast.187), channel_id=1, replica_groups=mesh['expert'=16,'tensor'=2] {'expert'}, dimensions={0} | all-to-all | bytes 21626880 | tf_op jit(solution)/shard_map/all_to_all | solution.py:45
  561.5 20.1 multiply_convert_fusion
  603.9 125.0 %reduce-scatter.14.cloned.1.call-done = bf16[16,220,768]{2,0,1:T(8,128)(2,1)} async-done(((bf16[16,440,768]{2,0,1:T(8,128)(2,1)}), bf16[16,220,768]{2,0,1:T(8,128)(2,1)}) %reduce-scatter.14.cloned.1.call-update) | async-done | bytes 5406736 | tf_op jit(solution)/shard_map/reduce_scatter | solution.py:50
  729.2 134.4 %all-gather.3.cloned.1.call-done = bf16[16,440,768]{2,0,1:T(8,128)(2,1)} async-done(((bf16[16,220,768]{2,0,1:T(8,128)(2,1)}), bf16[16,440,768]{2,0,1:T(8,128)(2,1)}) %all-gather.3.cloned.1.call-update) | async-done | bytes 10813456 | tf_op jit(solution)/shard_map/all_gather | solution.py:53
  876.2 36.2 %fusion.130 = (bf16[1,440,768]{2,0,1:T(2,128)(2,1)}, bf16[1,440,768]{2,0,1:T(2,128)(2,1)}, bf16[1,440,768]{2,0,1:T(2,128)(2,1)}, bf16[1,440,768]{2,0,1:T(2,128)(...) fusion(bf16[16,440,768]{2,0,1:T(8,128)(2,1)} %fusion.12), kind=kLoop, calls=%fused_computation.282 | loop fusion | bytes 21626880 | tf_op jit(solution)/shard_map/slice | solution.py:16
  995.5 133.6 %psum.52 = f32[]{:T(128)} all-reduce(f32[]{:T(128)S(6)} %mul_shard_map.3), channel_id=1, replica_groups=mesh['expert'=16,'tensor'=2] {'expert'}, use_global_device_ids=true, to_apply=%region_27.29 | all-reduce | flops 1 | bytes 8 | tf_op jit(solution)/shard_map/psum | solution.py:159
  1180.0 36.1 %collective-permute-done.10 = bf16[1,440,768]{2,1,0:T(8,128)(2,1)} collective-permute-done((bf16[1,440,768]{2,1,0:T(8,128)(2,1)}, bf16[1,440,768]{2,1,0:T(8,128)(2,1)}, u32[]{:S(2)}, u32[]{:S(2)}) %collective-permute-start.10) | collective-permute-done | bytes 675872 | tf_op jit(solution)/shard_map/ppermute | solution.py:19
  1232.4 57.8 %concatenate.31 = bf16[16,440,768]{2,0,1:T(8,128)(2,1)} concatenate(bf16[1,440,768]{2,0,1:T(2,128)(2,1)} %copy.314, bf16[1,440,768]{2,0,1:T(2,128)(2,1)} %copy.315, bf16[1,440,768]{2,0,1:T(2,128)(2,1)} %copy.316, bf16[1,440,768]{2,0,1:T(2,128)(2,1)} %copy.317, bf16[1,440,768]{2,0,1:T(2,128)(2,1)} %copy.318, bf16[1,440,768]{2,0,1:T(2,128)(2,1)} %copy.319, ...), dimensions={0} | concatenate | bytes 21626880 | tf_op jit(solution)/shard_map/concatenate | solution.py:20
  1307.1 25.2 reshape.457
  1332.3 86.4 %reduce_sum.387 = f32[8,440,768]{2,0,1:T(8,128)} reduce(f32[8,2,440,768]{3,1,0,2:T(2,128)} %reshape.457, f32[]{:T(128)} %constant.48.clone.1), dimensions={1}, to_apply=%region_24.26 | reduce | flops 2703360 | bytes 32440324 | tf_op jit(solution)/shard_map/reduce_sum | solution.py:57
  1499.3 238.1 %all_to_all.11 = bf16[16,440,768]{2,1,0:T(8,128)(2,1)S(1)} all-to-all(bf16[16,440,768]{2,1,0:T(8,128)(2,1)S(1)} %bitcast.188), channel_id=1, replica_groups=mesh['expert'=16,'tensor'=2] {'expert'}, dimensions={0} | all-to-all | bytes 21626880 | tf_op jit(solution)/shard_map/all_to_all | solution.py:45
  1737.4 28.2 fusion.6
  1788.0 124.3 %reduce-scatter.16.cloned.1.call-done = bf16[16,220,768]{2,0,1:T(8,128)(2,1)} async-done(((bf16[16,440,768]{2,0,1:T(8,128)(2,1)}), bf16[16,220,768]{2,0,1:T(8,128)(2,1)}) %reduce-scatter.16.cloned.1.call-update) | async-done | bytes 5406736 | tf_op jit(solution)/shard_map/reduce_scatter | solution.py:50
  1912.3 134.6 %all-gather.5.cloned.1.call-done = bf16[16,440,768]{2,0,1:T(8,128)(2,1)} async-done(((bf16[16,220,768]{2,0,1:T(8,128)(2,1)}), bf16[16,440,768]{2,0,1:T(8,128)(2,1)}) %all-gather.5.cloned.1.call-update) | async-done | bytes 10813456 | tf_op jit(solution)/shard_map/all_gather | solution.py:53
  2059.8 36.8 %fusion.129 = (bf16[1,440,768]{2,0,1:T(2,128)(2,1)}, bf16[1,440,768]{2,0,1:T(2,128)(2,1)}, bf16[1,440,768]{2,0,1:T(2,128)(2,1)}, bf16[1,440,768]{2,0,1:T(2,128)(...) fusion(bf16[16,440,768]{2,0,1:T(8,128)(2,1)} %fusion.9), kind=kLoop, calls=%fused_computation.281 | loop fusion | bytes 21626880 | tf_op jit(solution)/shard_map/slice | solution.py:16
  2193.0 44.8 %collective-permute-start.25 = (bf16[1,440,768]{2,1,0:T(8,128)(2,1)S(1)}, bf16[1,440,768]{2,1,0:T(8,128)(2,1)S(1)}, u32[]{:S(2)}, u32[]{:S(2)}) collective-permute-start(bf16[1,440,768]{2,1,0:T(8,128)(2,1)S(1)} %copy.341), channel_id=1, source_target_pairs={{0,10},{2,12},{4,14},{6,16},{8,18},{10,20},{12,22},{14,24},{16,26}... | collective-permute-start | bytes 2027528 | tf_op jit(solution)/shard_map/ppermute | solution.py:19
  2237.8 29.1 collective-permute-start.26
  2266.9 63.7 %collective-permute-done.22 = bf16[1,440,768]{2,1,0:T(8,128)(2,1)} collective-permute-done((bf16[1,440,768]{2,1,0:T(8,128)(2,1)}, bf16[1,440,768]{2,1,0:T(8,128)(2,1)}, u32[]{:S(2)}, u32[]{:S(2)}) %collective-permute-start.22) | collective-permute-done | bytes 675872 | tf_op jit(solution)/shard_map/ppermute | solution.py:19
  2373.3 57.8 %concatenate.32 = bf16[16,440,768]{2,0,1:T(8,128)(2,1)} concatenate(bf16[1,440,768]{2,0,1:T(2,128)(2,1)} %copy.346, bf16[1,440,768]{2,0,1:T(2,128)(2,1)} %copy.347, bf16[1,440,768]{2,0,1:T(2,128)(2,1)} %copy.348, bf16[1,440,768]{2,0,1:T(2,128)(2,1)} %copy.349, bf16[1,440,768]{2,0,1:T(2,128)(2,1)} %copy.350, bf16[1,440,768]{2,0,1:T(2,128)(2,1)} %copy.351, ...), dimensions={0} | concatenate | bytes 21626880 | tf_op jit(solution)/shard_map/concatenate | solution.py:20
  2448.0 25.3 reshape.458
  2473.3 86.6 %reduce_sum.393 = f32[8,440,768]{2,0,1:T(8,128)} reduce(f32[8,2,440,768]{3,1,0,2:T(2,128)} %reshape.458, f32[]{:T(128)} %constant.48.clone.1), dimensions={1}, to_apply=%region_29.31 | reduce | flops 2703360 | bytes 32440324 | tf_op jit(solution)/shard_map/reduce_sum | solution.py:57
  2657.6 57.5 %all-reduce.19.cloned.1.call-done = bf16[1182,768]{1,0:T(8,128)(2,1)} async-done(((bf16[1182,768]{1,0:T(8,128)(2,1)}), bf16[1182,768]{1,0:T(8,128)(2,1)}) %all-reduce.19.cloned.1.call-update) | async-done | bytes 1815568 | tf_op jit(solution)/shard_map/psum | solution.py:40
  2737.5 57.0 %all-reduce.21.cloned.1.call-done = bf16[1182,768]{1,0:T(8,128)(2,1)} async-done(((bf16[1182,768]{1,0:T(8,128)(2,1)}), bf16[1182,768]{1,0:T(8,128)(2,1)}) %all-reduce.21.cloned.1.call-update) | async-done | bytes 1815568 | tf_op jit(solution)/shard_map/psum | solution.py:40
  2883.9 33.6 all-reduce.23.cloned.1.call-done
  3007.9 29.6 all-reduce.1
  3044.2 50.1 %reduce-scatter.22.cloned.1.call-done = f32[48,4]{1,0:T(8,128)} async-done(((f32[768,4]{1,0:T(8,128)}), f32[48,4]{1,0:T(8,128)}) %reduce-scatter.22.cloned.1.call-update) | async-done | bytes 784
  3095.7 186.8 %all-reduce.25.cloned.1.call-done = (f32[2,3,768,384]{3,0,1,2:T(2,128)}, f32[2,384,768]{1,0,2:T(2,128)}) async-done(((f32[2,3,768,384]{3,0,1,2:T(2,128)}, f32[2,384,768]{1,0,2:T(2,128)}), (f32[2,3,768,384]{3,0,1,2:T(2,128)}, f32[2,384,768]{1,0,2:T(2,128)})) %all-reduce.25.cloned.1.call-update) | async-done | bytes 9437200
  3286.1 76.4 %reduce-scatter.20.cloned.1.call-done = f32[1536,48]{0,1:T(8,128)} async-done(((f32[1536,768]{0,1:T(8,128)}), f32[1536,48]{0,1:T(8,128)}) %reduce-scatter.20.cloned.1.call-update) | async-done | bytes 294928 | tf_op jit(solution)/shard_map/reduce_scatter | solution.py:267
  3362.5 79.4 %reduce-scatter.18.cloned.1.call-done = f32[48,1536]{1,0:T(8,128)} async-done(((f32[768,1536]{1,0:T(8,128)}), f32[48,1536]{1,0:T(8,128)}) %reduce-scatter.18.cloned.1.call-update) | async-done | bytes 294928 | tf_op jit(solution)/shard_map/reduce_scatter | solution.py:266
  (689 shorter events, 939.3 us)
Async XLA Ops:
  7.2 108.3 %all-reduce.13.cloned.1.call-start = ((), (), s32[]{:S(2)}) async-start(), calls=%async_computation.9 | async-start | bytes 3637248 | tf_op jit(solution)/shard_map/psum | solution.py:40
  55.9 133.0 %all-reduce.15.cloned.1.call-start = ((), (), s32[]{:S(2)}) async-start(), calls=%async_computation.10 | async-start | bytes 3637248 | tf_op jit(solution)/shard_map/psum | solution.py:40
  131.9 162.9 %all-reduce.17.cloned.1.call-start = ((), (), s32[]{:S(2)}) async-start(), calls=%async_computation.11 | async-start | bytes 3637248 | tf_op jit(solution)/shard_map/psum | solution.py:40
  237.8 491.2 %reduce-scatter.14.cloned.1.call-start = ((), (), s32[]{:S(2)}) async-start(), calls=%async_computation.12 | async-start | bytes 16220160 | tf_op jit(solution)/shard_map/reduce_scatter | solution.py:50
  603.9 259.7 %all-gather.3.cloned.1.call-start = ((), (), s32[]{:S(2)}) async-start(), calls=%async_computation.13 | async-start | bytes 16220160 | tf_op jit(solution)/shard_map/all_gather | solution.py:53
  729.0 1183.3 %reduce-scatter.16.cloned.1.call-start = ((), (), s32[]{:S(2)}) async-start(), calls=%async_computation.14 | async-start | bytes 16220160 | tf_op jit(solution)/shard_map/reduce_scatter | solution.py:50
  936.3 202.2 %collective-permute-start.5 = (bf16[1,440,768]{2,1,0:T(8,128)(2,1)}, bf16[1,440,768]{2,1,0:T(8,128)(2,1)}, u32[]{:S(2)}, u32[]{:S(2)}) collective-permute-start(bf16[1,440,768]{2,1,0:T(8,128)(2,1)} %copy.304), channel_id=1, source_target_pairs={{0,20},{2,22},{4,24},{6,26},{8,28},{10,30},{12,0},{14,2},{16,4},{1... | collective-permute-start | bytes 2027528 | tf_op jit(solution)/shard_map/ppermute | solution.py:19
  950.8 191.4 %collective-permute-start.6 = (bf16[1,440,768]{2,1,0:T(8,128)(2,1)}, bf16[1,440,768]{2,1,0:T(8,128)(2,1)}, u32[]{:S(2)}, u32[]{:S(2)}) collective-permute-start(bf16[1,440,768]{2,1,0:T(8,128)(2,1)} %copy.305), channel_id=1, source_target_pairs={{0,18},{2,20},{4,22},{6,24},{8,26},{10,28},{12,30},{14,0},{16,2},{... | collective-permute-start | bytes 2027528 | tf_op jit(solution)/shard_map/ppermute | solution.py:19
  965.3 178.3 %collective-permute-start.7 = (bf16[1,440,768]{2,1,0:T(8,128)(2,1)}, bf16[1,440,768]{2,1,0:T(8,128)(2,1)}, u32[]{:S(2)}, u32[]{:S(2)}) collective-permute-start(bf16[1,440,768]{2,1,0:T(8,128)(2,1)} %copy.306), channel_id=1, source_target_pairs={{0,16},{2,18},{4,20},{6,22},{8,24},{10,26},{12,28},{14,30},{16,0},... | collective-permute-start | bytes 2027528 | tf_op jit(solution)/shard_map/ppermute | solution.py:19
  979.8 168.2 %collective-permute-start.8 = (bf16[1,440,768]{2,1,0:T(8,128)(2,1)}, bf16[1,440,768]{2,1,0:T(8,128)(2,1)}, u32[]{:S(2)}, u32[]{:S(2)}) collective-permute-start(bf16[1,440,768]{2,1,0:T(8,128)(2,1)} %copy.307), channel_id=1, source_target_pairs={{0,14},{2,16},{4,18},{6,20},{8,22},{10,24},{12,26},{14,28},{16,30}... | collective-permute-start | bytes 2027528 | tf_op jit(solution)/shard_map/ppermute | solution.py:19
  994.3 153.8 %collective-permute-start.9 = (bf16[1,440,768]{2,1,0:T(8,128)(2,1)}, bf16[1,440,768]{2,1,0:T(8,128)(2,1)}, u32[]{:S(2)}, u32[]{:S(2)}) collective-permute-start(bf16[1,440,768]{2,1,0:T(8,128)(2,1)} %copy.308), channel_id=1, source_target_pairs={{0,12},{2,14},{4,16},{6,18},{8,20},{10,22},{12,24},{14,26},{16,28}... | collective-permute-start | bytes 2027528 | tf_op jit(solution)/shard_map/ppermute | solution.py:19
  1138.6 77.5 %collective-permute-start.10 = (bf16[1,440,768]{2,1,0:T(8,128)(2,1)}, bf16[1,440,768]{2,1,0:T(8,128)(2,1)}, u32[]{:S(2)}, u32[]{:S(2)}) collective-permute-start(bf16[1,440,768]{2,1,0:T(8,128)(2,1)} %copy.309), channel_id=1, source_target_pairs={{0,10},{2,12},{4,14},{6,16},{8,18},{10,20},{12,22},{14,24},{16,26}... | collective-permute-start | bytes 2027528 | tf_op jit(solution)/shard_map/ppermute | solution.py:19
  1142.2 77.3 %collective-permute-start.11 = (bf16[1,440,768]{2,1,0:T(8,128)(2,1)}, bf16[1,440,768]{2,1,0:T(8,128)(2,1)}, u32[]{:S(2)}, u32[]{:S(2)}) collective-permute-start(bf16[1,440,768]{2,1,0:T(8,128)(2,1)} %copy.310), channel_id=1, source_target_pairs={{0,8},{2,10},{4,12},{6,14},{8,16},{10,18},{12,20},{14,22},{16,24},... | collective-permute-start | bytes 2027528 | tf_op jit(solution)/shard_map/ppermute | solution.py:19
  1143.6 79.0 %collective-permute-start.12 = (bf16[1,440,768]{2,1,0:T(8,128)(2,1)}, bf16[1,440,768]{2,1,0:T(8,128)(2,1)}, u32[]{:S(2)}, u32[]{:S(2)}) collective-permute-start(bf16[1,440,768]{2,1,0:T(8,128)(2,1)} %copy.311), channel_id=1, source_target_pairs={{0,6},{2,8},{4,10},{6,12},{8,14},{10,16},{12,18},{14,20},{16,22},{... | collective-permute-start | bytes 2027528 | tf_op jit(solution)/shard_map/ppermute | solution.py:19
  1148.0 77.9 %collective-permute-start.13 = (bf16[1,440,768]{2,1,0:T(8,128)(2,1)}, bf16[1,440,768]{2,1,0:T(8,128)(2,1)}, u32[]{:S(2)}, u32[]{:S(2)}) collective-permute-start(bf16[1,440,768]{2,1,0:T(8,128)(2,1)} %copy.312), channel_id=1, source_target_pairs={{0,4},{2,6},{4,8},{6,10},{8,12},{10,14},{12,16},{14,18},{16,20},{1... | collective-permute-start | bytes 2027528 | tf_op jit(solution)/shard_map/ppermute | solution.py:19
  1148.0 81.2 %collective-permute-start.14 = (bf16[1,440,768]{2,1,0:T(8,128)(2,1)}, bf16[1,440,768]{2,1,0:T(8,128)(2,1)}, u32[]{:S(2)}, u32[]{:S(2)}) collective-permute-start(bf16[1,440,768]{2,1,0:T(8,128)(2,1)} %copy.313), channel_id=1, source_target_pairs={{0,2},{2,4},{4,6},{6,8},{8,10},{10,12},{12,14},{14,16},{16,18},{18... | collective-permute-start | bytes 2027528 | tf_op jit(solution)/shard_map/ppermute | solution.py:19
  1787.9 259.0 %all-gather.5.cloned.1.call-start = ((), (), s32[]{:S(2)}) async-start(), calls=%async_computation.15 | async-start | bytes 16220160 | tf_op jit(solution)/shard_map/all_gather | solution.py:53
  1912.3 802.8 %all-reduce.19.cloned.1.call-start = ((), (), s32[]{:S(2)}) async-start(), calls=%async_computation.16 | async-start | bytes 3637248 | tf_op jit(solution)/shard_map/psum | solution.py:40
  2135.0 102.8 %collective-permute-start.21 = (bf16[1,440,768]{2,1,0:T(8,128)(2,1)}, bf16[1,440,768]{2,1,0:T(8,128)(2,1)}, u32[]{:S(2)}, u32[]{:S(2)}) collective-permute-start(bf16[1,440,768]{2,1,0:T(8,128)(2,1)} %copy.337), channel_id=1, source_target_pairs={{0,18},{2,20},{4,22},{6,24},{8,26},{10,28},{12,30},{14,0},{16,2},{... | collective-permute-start | bytes 2027528 | tf_op jit(solution)/shard_map/ppermute | solution.py:19
  2149.4 181.2 %collective-permute-start.22 = (bf16[1,440,768]{2,1,0:T(8,128)(2,1)}, bf16[1,440,768]{2,1,0:T(8,128)(2,1)}, u32[]{:S(2)}, u32[]{:S(2)}) collective-permute-start(bf16[1,440,768]{2,1,0:T(8,128)(2,1)} %copy.338), channel_id=1, source_target_pairs={{0,16},{2,18},{4,20},{6,22},{8,24},{10,26},{12,28},{14,30},{16,0},... | collective-permute-start | bytes 2027528 | tf_op jit(solution)/shard_map/ppermute | solution.py:19
  2163.9 166.8 %collective-permute-start.23 = (bf16[1,440,768]{2,1,0:T(8,128)(2,1)}, bf16[1,440,768]{2,1,0:T(8,128)(2,1)}, u32[]{:S(2)}, u32[]{:S(2)}) collective-permute-start(bf16[1,440,768]{2,1,0:T(8,128)(2,1)} %copy.339), channel_id=1, source_target_pairs={{0,14},{2,16},{4,18},{6,20},{8,22},{10,24},{12,26},{14,28},{16,30}... | collective-permute-start | bytes 2027528 | tf_op jit(solution)/shard_map/ppermute | solution.py:19
  2178.4 152.3 %collective-permute-start.24 = (bf16[1,440,768]{2,1,0:T(8,128)(2,1)}, bf16[1,440,768]{2,1,0:T(8,128)(2,1)}, u32[]{:S(2)}, u32[]{:S(2)}) collective-permute-start(bf16[1,440,768]{2,1,0:T(8,128)(2,1)} %copy.340), channel_id=1, source_target_pairs={{0,12},{2,14},{4,16},{6,18},{8,20},{10,22},{12,24},{14,26},{16,28}... | collective-permute-start | bytes 2027528 | tf_op jit(solution)/shard_map/ppermute | solution.py:19
  2193.0 169.4 %collective-permute-start.25 = (bf16[1,440,768]{2,1,0:T(8,128)(2,1)S(1)}, bf16[1,440,768]{2,1,0:T(8,128)(2,1)S(1)}, u32[]{:S(2)}, u32[]{:S(2)}) collective-permute-start(bf16[1,440,768]{2,1,0:T(8,128)(2,1)S(1)} %copy.341), channel_id=1, source_target_pairs={{0,10},{2,12},{4,14},{6,16},{8,18},{10,20},{12,22},{14,24},{16,26}... | collective-permute-start | bytes 2027528 | tf_op jit(solution)/shard_map/ppermute | solution.py:19
  2237.8 126.9 %collective-permute-start.26 = (bf16[1,440,768]{2,1,0:T(8,128)(2,1)S(1)}, bf16[1,440,768]{2,1,0:T(8,128)(2,1)S(1)}, u32[]{:S(2)}, u32[]{:S(2)}) collective-permute-start(bf16[1,440,768]{2,1,0:T(8,128)(2,1)S(1)} %copy.342), channel_id=1, source_target_pairs={{0,8},{2,10},{4,12},{6,14},{8,16},{10,18},{12,20},{14,22},{16,24},... | collective-permute-start | bytes 2027528 | tf_op jit(solution)/shard_map/ppermute | solution.py:19
  2657.5 136.9 %all-reduce.21.cloned.1.call-start = ((), (), s32[]{:S(2)}) async-start(), calls=%async_computation.17 | async-start | bytes 3637248 | tf_op jit(solution)/shard_map/psum | solution.py:40
  2737.4 180.1 %all-reduce.23.cloned.1.call-start = ((), (), s32[]{:S(2)}) async-start(), calls=%async_computation.18 | async-start | bytes 3637248 | tf_op jit(solution)/shard_map/psum | solution.py:40
  2860.5 116.7 %reduce-scatter.26.cloned.1.call-start = ((), (), s32[]{:S(2)}) async-start(), calls=%async_computation.23 | async-start | bytes 417792
  2863.5 179.3 %reduce-scatter.24.cloned.1.call-start = ((), (), s32[]{:S(2)}) async-start(), calls=%async_computation.22 | async-start | bytes 417792
  2927.1 167.2 %reduce-scatter.22.cloned.1.call-start = ((), (), s32[]{:S(2)}) async-start(), calls=%async_computation.21 | async-start | bytes 417792
  2930.1 352.4 %all-reduce.25.cloned.1.call-start = ((), (), s32[]{:S(2)}) async-start(), calls=%async_computation.24 | async-start | bytes 18874368
  2952.0 410.4 %reduce-scatter.20.cloned.1.call-start = ((), (), s32[]{:S(2)}) async-start(), calls=%async_computation.20 | async-start | bytes 5013504 | tf_op jit(solution)/shard_map/reduce_scatter | solution.py:267
  2962.0 479.8 %reduce-scatter.18.cloned.1.call-start = ((), (), s32[]{:S(2)}) async-start(), calls=%async_computation.19 | async-start | bytes 5013504 | tf_op jit(solution)/shard_map/reduce_scatter | solution.py:266
  (179 other events, 4911.7 us)
Sparse Core Ops, SparseCore 0:
  56.0 59.5 all-reduce.12
  132.0 56.8 all-reduce.14
  237.9 56.8 all-reduce.16
  604.0 124.8 reduce-scatter.13
  730.4 133.0 all-gather.2
  1788.0 124.1 reduce-scatter.15
  1913.8 133.1 all-gather.4
  2657.6 57.4 all-reduce.18
  2737.6 56.8 all-reduce.20
  2860.6 56.8 all-reduce.22
  2921.6 55.5 reduce-scatter.25
  2981.0 54.5 reduce-scatter.23
  3039.6 54.6 reduce-scatter.21
  3098.3 184.1 all-reduce.24
  3286.8 75.6 reduce-scatter.19
  3367.2 74.5 reduce-scatter.17
